TPU v7x, 512 devices: a whole 4x8x8 slice. The times are simulated.
512 devices in a mesh: dp: 4 (over x), tensor: 128 (over z, y, core).
Axes of the slice: x: 4, y: 8, z: 8, core: 2. Of those that a mesh axis runs over, the one named last changes fastest.
Arguments:
- hidden: bfloat16 [8192, 2048], P(('dp', 'tensor')), may hold values from -6 to 6
- norm_gain: float32 [2048], replicated, may hold values from 0.5 to 1.5
- head_weight: bfloat16 [2048, 102400], P('dp', 'tensor'), as said below
- token_ids: int32 [8192], P(('dp', 'tensor')), may hold values from 0 to 102399
- lengths: int32 [4, 4], P('dp'), may hold values from 1 to 512, 1024 in all within a row
Outputs:
- logprob: float32 [8192], P(('dp', 'tensor'))
- entropy: float32 [8192], P(('dp', 'tensor'))
Inputs may be any that keep to these rules, and one draw needn't show every extreme that they name: Each index of dp has 4 lengths that sum to exactly 1024, and one of them equals 512. `head_weight`: head weights.
All inputs are finite; a program needn't handle non-finite values.
Results may differ from a plain program's by a relative error of at most 0.0045.
Values may be sent and summed in bfloat16 or wider, within the bound.
No kernel may reach another device: no remote copies, remote signals or barrier semaphores. Data moves between devices by JAX's collectives and lax.ppermute only.
A program may use at most 64 MiB of HBM per device.

v0:
```python
import jax
import jax.numpy as jnp
from jax import lax
from jax.sharding import PartitionSpec as P

SEQ_DP = 4
SLOT = 512


def per_device(hidden, norm_gain, head_weight, token_ids, lengths):
    row_dev = hidden.shape[0]
    tensor_idx = lax.axis_index("tensor")
    wide = hidden.astype(jnp.float32)
    meansq = jnp.mean(wide * wide, axis=-1, keepdims=True)
    normed = (wide * lax.rsqrt(meansq + 1e-06) * norm_gain).astype(jnp.bfloat16)
    weight = lax.all_gather(head_weight, "dp", axis=0, tiled=True)
    vocab_dev = weight.shape[1]
    vstart = tensor_idx * vocab_dev
    seq_len = lengths[0]
    seq_iota = jnp.arange(SEQ_DP, dtype=jnp.int32)
    vocab_iota = jnp.arange(vocab_dev, dtype=jnp.int32)
    own_rows = tensor_idx * row_dev + jnp.arange(row_dev, dtype=jnp.int32)
    logits = jnp.dot(
        lax.all_gather(normed, "tensor", axis=0, tiled=True),
        weight,
        preferred_element_type=jnp.float32,
    )
    top = jnp.max(logits, axis=1)
    expo = jnp.exp(logits - top[:, None])
    total = jnp.sum(expo, axis=1)
    moment = jnp.sum(expo * logits, axis=1)
    hit = (lax.all_gather(token_ids, "tensor", axis=0, tiled=True) - vstart)[:, None] == vocab_iota[
        None, :
    ]
    chosen = jnp.sum(jnp.where(hit, logits, 0.0), axis=1)
    fresh = (top, total, moment, chosen)
    top, total, moment, chosen = tuple((new for new in fresh))
    onehot = (own_rows // SLOT)[:, None] == seq_iota[None, :]
    length_of = jnp.sum(jnp.where(onehot, seq_len[None, :], 0), axis=1)
    within = own_rows % SLOT
    scored = within < length_of
    top_all = lax.pmax(top, "tensor")
    rescale = jnp.exp(top - top_all)
    top_own = top_all[own_rows]
    total_all, moment_all, chosen_all = lax.psum(
        (total * rescale, moment * rescale, chosen), "tensor"
    )
    total_own, moment_own, chosen_own = (
        total_all[own_rows],
        moment_all[own_rows],
        chosen_all[own_rows],
    )
    safe_total = jnp.where(scored, total_own, 1.0)
    lse = top_own + jnp.log(safe_total)
    logprob = jnp.where(scored, chosen_own - lse, 0.0)
    entropy = jnp.where(scored, lse - moment_own / safe_total, 0.0)
    return (logprob, entropy)


def solution(mesh):
    return jax.shard_map(
        per_device,
        mesh=mesh,
        in_specs=(
            P(("dp", "tensor"), None),
            P(),
            P("dp", "tensor"),
            P(("dp", "tensor")),
            P("dp", None),
        ),
        out_specs=(P(("dp", "tensor")), P(("dp", "tensor"))),
        check_vma=False,
    )
```

profile of v0, /device:TPU:2, one launch (start us, length us, event | category | flops | bytes accessed | tf_op | source)
XLA Modules:
  0.0 923.0 jit_solution(2070822759771183285)
XLA Ops:
  7.2 0.0 all-gather.5.cloned.1.call-start
  7.2 0.7 all-gather.5.cloned.1.call-update
  7.9 0.0 all-gather.3.cloned.1.call-start
  7.9 1.0 fusion.1
  8.9 1.6 fusion.3
  10.5 0.0 all-gather.3.cloned.1.call-update
  10.5 1.3 dynamic-slice
  12.5 0.9 dynamic-update-slice
  13.3 32.3 %all-reduce = s32[2048]{0:T(1024)S(1)} all-reduce(s32[2048]{0:T(1024)S(1)} %dynamic-update-slice), channel_id=1, replica_groups=mesh['dp'=4,'tensor'=128] {'tensor'}, use_global_device_ids=true, to_apply=%add | all-reduce | flops 2048 | bytes 16384
  45.6 0.7 select_reduce_fusion.1
  46.4 13.6 %all-gather.5.cloned.1.call-done = bf16[2048,800]{0,1:T(8,128)(2,1)} async-done(((bf16[512,800]{0,1:T(8,128)(2,1)}), bf16[2048,800]{0,1:T(8,128)(2,1)}) %all-gather.5.cloned.1.call-update) | async-done | bytes 3276816 | tf_op jit(solution)/shard_map/all_gather | solution.py:16
  60.0 92.3 %all-gather.3.cloned.1.call-done = bf16[2048,2048]{1,0:T(8,128)(2,1)} async-done(((bf16[16,2048]{1,0:T(8,128)(2,1)}), bf16[2048,2048]{1,0:T(8,128)(2,1)}) %all-gather.3.cloned.1.call-update) | async-done | bytes 8388624 | tf_op jit(solution)/shard_map/all_gather | solution.py:24
  152.3 12.1 %fusion.8 = (f32[2048]{0:T(1024)S(1)}, f32[2048,800]{0,1:T(8,128)}) fusion(bf16[2048,2048]{1,0:T(8,128)(2,1)} %all-gather.3.cloned.1.call-done, bf16[2048,800]{0,1:T(8,128)(2,1)} %all-gather.5.cloned.1.call-done), kind=kOutput, calls=%fused_computation.35 | convolution fusion | flops 6712522752 | bytes 18227200 | tf_op jit(solution)/shard_map/dot_general | solution.py:23
  164.3 253.6 %pmax.7 = f32[2048]{0:T(1024)S(1)} all-reduce(f32[2048]{0:T(1024)S(1)} %get-tuple-element.12), channel_id=1, replica_groups=mesh['dp'=4,'tensor'=128] {'tensor'}, use_global_device_ids=true, to_apply=%region_5.6 | all-reduce | flops 2048 | bytes 16384 | tf_op jit(solution)/shard_map/pmax | solution.py:42
  417.9 4.1 multiply_reduce_fusion
  422.0 0.7 gather_fusion.1
  422.7 490.9 %all-reduce.1 = (f32[2048]{0:T(1024)S(1)}, f32[2048]{0:T(1024)S(1)}, f32[2048]{0:T(1024)S(1)}) all-reduce(f32[2048]{0:T(1024)S(1)} %get-tuple-element.4, f32[2048]{0:T(1024)S(1)} %get-tuple-element.9, f32[2048]{0:T(1024)S(1)} %get-tuple-element.8), channel_id=1, replica_groups=mesh['dp'=4,'tensor'=128] {'tensor'}, use_global_device_ids=true, to_apply=%region_3.0 | all-reduce | flops 6144 | bytes 49152 | tf_op jit(solution)/shard_map/psum | solution.py:45
  913.6 0.7 gather_fusion
  914.3 0.7 gather_fusion.2
  914.9 0.7 gather_fusion.3
  915.6 0.5 subtract_select_fusion
  (7 shorter events, 0.0 us)
Async XLA Ops:
  7.2 52.8 %all-gather.5.cloned.1.call-start = ((), (), s32[]{:S(2)}) async-start(), calls=%async_computation.1 | async-start | bytes 4096000 | tf_op jit(solution)/shard_map/all_gather | solution.py:16
  7.9 144.4 %all-gather.3.cloned.1.call-start = ((), (), s32[]{:S(2)}) async-start(), calls=%async_computation | async-start | bytes 8454144 | tf_op jit(solution)/shard_map/all_gather | solution.py:24
Sparse Core Ops, SparseCore 0:
  10.1 49.8 all-gather.4
  63.1 89.1 all-gather.2
where the time goes:
time: 923 us
  blocking collectives  777 us (84%)
  waiting for transfers between devices  107 us (12%)
  between operations  14.7 us (2%)
  matrix products  12.1 us (1%)
    psum x1, blocking collectives, per_device(): lax.psum((total * rescale, moment * rescale, chosen), 'tensor')  491 us
    pmax x1, blocking collectives, per_device(): top_all = lax.pmax(top, 'tensor')  254 us
    all_gather x1, waiting for transfers between devices, per_device(): lax.all_gather(normed, 'tensor', axis=0, tiled=True)  92.3 us
    unnamed x1, blocking collectives  32.3 us
  transfers between devices with their start and end apart: 2, of which 2 were waited for; matrix products, arithmetic and copies ran while one was open for 1% of the time, Pallas kernels for 0%

commit v1 on v0

--- a/solution.py
+++ b/solution.py
@@ -5,6 +5,11 @@
 
 SEQ_DP = 4
 SLOT = 512
+
+
+def exchange_gather(array, axis, along):
+    sent = jnp.stack([array] * lax.axis_size(axis))
+    return jnp.concatenate(lax.all_to_all(sent, axis, 0, 0), axis=along)
 
 
 def per_device(hidden, norm_gain, head_weight, token_ids, lengths):
@@ -21,9 +26,7 @@
     vocab_iota = jnp.arange(vocab_dev, dtype=jnp.int32)
     own_rows = tensor_idx * row_dev + jnp.arange(row_dev, dtype=jnp.int32)
     logits = jnp.dot(
-        lax.all_gather(normed, "tensor", axis=0, tiled=True),
-        weight,
-        preferred_element_type=jnp.float32,
+        exchange_gather(normed, "tensor", 0), weight, preferred_element_type=jnp.float32
     )
     top = jnp.max(logits, axis=1)
     expo = jnp.exp(logits - top[:, None])

time: 923 us -> 1070 us (1.16)
  blocking collectives: 777 us -> 1010 us
  waiting for transfers between devices: 107 us -> 0.7 us
  starting transfers between devices: 0.08 us -> 18.5 us
    unnamed x1, blocking collectives: 32.3 us -> 250 us
    all_gather x1 -> x0, waiting for transfers between devices: 92.3 us -> none  [per_device(): lax.all_gather(normed, 'tensor', axis=0, tiled=True)]
    all_to_all x0 -> x1, starting transfers between devices: none -> 18.5 us  [exchange_gather(): return jnp.concatenate(lax.all_to_all(sent, axis, 0, 0), axis=along)]
    all_gather x1, waiting for transfers between devices: 13.6 us -> 0.02 us  [per_device(): weight = lax.all_gather(head_weight, 'dp', axis=0, tiled=True)]
    pmax x1, blocking collectives: 254 us -> 265 us  [per_device(): top_all = lax.pmax(top, 'tensor')]
  transfers between devices with their start and end apart: 2 -> 2, of which waited for: 2 -> 0; matrix products, arithmetic and copies ran while one was open for 1% -> 0% of each run, Pallas kernels for 0% -> 0%
where the time goes in v1:
time: 1070 us
  blocking collectives  1010 us (94%)
  starting transfers between devices  18.5 us (2%)
  between operations  14.8 us (1%)
  matrix products  12.1 us (1%)
    psum x1, blocking collectives, per_device(): lax.psum((total * rescale, moment * rescale, chosen), 'tensor')  491 us
    pmax x1, blocking collectives, per_device(): top_all = lax.pmax(top, 'tensor')  265 us
    unnamed x1, blocking collectives  250 us
  transfers between devices with their start and end apart: 2, of which 0 were waited for; matrix products, arithmetic and copies ran while one was open for 0% of the time, Pallas kernels for 0%

profile of v1, /device:TPU:2, one launch (start us, length us, event | category | flops | bytes accessed | tf_op | source)
XLA Modules:
  0.0 1067.5 jit_solution(5954348087897906832)
XLA Ops:
  7.2 1.0 fusion.1
  8.1 0.9 fusion.3
  9.1 4.3 stack.2
  13.3 0.0 copy-start
  13.4 0.0 copy-start.1
  13.4 18.5 %all-to-all-start = ((bf16[128,16,2048]{2,1,0:T(8,128)(2,1)}), bf16[128,16,2048]{2,1,0:T(8,128)(2,1)}, u32[]{:S(2)}, u32[]{:S(2)}) async-start(bf16[128,16,2048]{2,1,0:T(8,128)(2,1)} %stack.2), calls=%async_computation | async-start | bytes 16777216 | tf_op jit(solution)/shard_map/all_to_all | solution.py:12
  31.8 0.0 all-gather.2.cloned.1.call-start
  31.9 0.7 all-gather.2.cloned.1.call-update
  32.6 1.3 dynamic-slice
  34.5 0.0 copy-done
  34.5 0.3 dynamic-update-slice
  34.8 250.1 %all-reduce = s32[2048]{0:T(1024)S(1)} all-reduce(s32[2048]{0:T(1024)S(1)} %dynamic-update-slice), channel_id=1, replica_groups=mesh['dp'=4,'tensor'=128] {'tensor'}, use_global_device_ids=true, to_apply=%add | all-reduce | flops 2048 | bytes 16384
  284.9 0.0 copy-done.1
  284.9 0.1 select_reduce_fusion.1
  285.0 0.0 all-gather.2.cloned.1.call-done
  285.0 0.0 all-to-all-done
  285.1 12.1 %fusion.8 = (f32[2048]{0:T(1024)S(1)}, f32[2048,800]{0,1:T(8,128)}) fusion(bf16[2048,2048]{1,0:T(8,128)(2,1)} %bitcast.2, bf16[2048,800]{0,1:T(8,128)(2,1)} %all-gather.2.cloned.1.call-done), kind=kOutput, calls=%fused_computation.35 | convolution fusion | flops 6712522752 | bytes 18227200 | tf_op jit(solution)/shard_map/dot_general | solution.py:28
  297.1 265.4 %pmax.7 = f32[2048]{0:T(1024)S(1)} all-reduce(f32[2048]{0:T(1024)S(1)} %get-tuple-element.12), channel_id=1, replica_groups=mesh['dp'=4,'tensor'=128] {'tensor'}, use_global_device_ids=true, to_apply=%region_5.6 | all-reduce | flops 2048 | bytes 16384 | tf_op jit(solution)/shard_map/pmax | solution.py:45
  562.5 4.1 multiply_reduce_fusion
  566.6 0.7 gather_fusion.1
  567.3 490.9 %all-reduce.1 = (f32[2048]{0:T(1024)S(1)}, f32[2048]{0:T(1024)S(1)}, f32[2048]{0:T(1024)S(1)}) all-reduce(f32[2048]{0:T(1024)S(1)} %get-tuple-element.4, f32[2048]{0:T(1024)S(1)} %get-tuple-element.9, f32[2048]{0:T(1024)S(1)} %get-tuple-element.8), channel_id=1, replica_groups=mesh['dp'=4,'tensor'=128] {'tensor'}, use_global_device_ids=true, to_apply=%region_3.0 | all-reduce | flops 6144 | bytes 49152 | tf_op jit(solution)/shard_map/psum | solution.py:48
  1058.2 0.7 gather_fusion
  1058.8 0.7 gather_fusion.2
  1059.5 0.7 gather_fusion.3
  1060.1 0.5 subtract_select_fusion
  (7 shorter events, 0.0 us)
Async XLA Ops:
  13.3 21.2 %copy-start = (s32[16]{0:T(128)S(1)}, s32[16]{0:T(128)}, u32[]{:S(2)}) copy-start(s32[16]{0:T(128)} %param.8) | copy-start | bytes 196
  13.4 271.6 %copy-start.1 = (s32[1,4]{1,0:T(1,128)S(1)}, s32[1,4]{1,0:T(1,128)}, u32[]{:S(2)}) copy-start(s32[1,4]{1,0:T(1,128)} %param.9) | copy-start | bytes 52
  13.4 271.7 %all-to-all-start = ((bf16[128,16,2048]{2,1,0:T(8,128)(2,1)}), bf16[128,16,2048]{2,1,0:T(8,128)(2,1)}, u32[]{:S(2)}, u32[]{:S(2)}) async-start(bf16[128,16,2048]{2,1,0:T(8,128)(2,1)} %stack.2), calls=%async_computation | async-start | bytes 16777216 | tf_op jit(solution)/shard_map/all_to_all | solution.py:12
  31.8 253.2 %all-gather.2.cloned.1.call-start = ((), (), s32[]{:S(2)}) async-start(), calls=%async_computation.1 | async-start | bytes 4096000 | tf_op jit(solution)/shard_map/all_gather | solution.py:21
Sparse Core Ops, SparseCore 0:
  34.8 45.6 all-gather.1
